TPU v7x, 32 devices: a whole 2x2x4 slice. The times are simulated.
32 devices in a mesh: grp: 8 (over z, y), tp: 2 (over core), fs: 2 (over x).
Axes of the slice: x: 2, y: 2, z: 4, core: 2. Of those that a mesh axis runs over, the one named last changes fastest.
Arguments:
- tokens: bfloat16 [512, 4, 8192], P('grp', None, ('tp', 'fs')), may hold values from -64 to 64
- norm_gain: bfloat16 [8192], P(('tp', 'fs')), may hold values from 0.25 to 1.75
- queries: bfloat16 [512, 4, 8192], P('grp', None, ('tp', 'fs')), may hold values from -64 to 64
- rotated_key_cache: bfloat16 [512, 32, 1024], P('grp', None, ('tp', 'fs')), may hold values from -6 to 6
- head_value_cache: bfloat16 [512, 32, 1024], P('grp', None, ('tp', 'fs')), may hold values from -6 to 6
- lengths: int32 [512], P('grp'), may hold values from 2 to 32
- master: float32 [8192, 2048], P('grp', ('tp', 'fs')), may hold values from -0.0625 to 0.0625
- moment_first: float32 [8192, 2048], P('grp', ('tp', 'fs')), may hold values from -4 to 4
- moment_second: float32 [8192, 2048], P('grp', ('tp', 'fs')), may hold values from 0.1 to 1
- gradient: float32 [8192, 2048], P('grp', ('tp', 'fs')), may hold values from -6 to 6
Outputs:
- attended: bfloat16 [512, 4, 8192], P('grp', None, ('tp', 'fs'))
- appended: bfloat16 [512, 4, 2048], P('grp', None, ('tp', 'fs'))
- new_master: float32 [8192, 2048], P('grp', ('tp', 'fs'))
- new_first: float32 [8192, 2048], P('grp', ('tp', 'fs'))
- new_second: float32 [8192, 2048], P('grp', ('tp', 'fs'))
All inputs are finite; a program needn't handle non-finite values.
Results may differ from a plain program's by a relative error of at most 0.0057.
Values may be sent and summed in bfloat16 or wider, within the bound.
A program may use at most 128 MiB of HBM per device.

v0:
```python
import jax
import jax.numpy as jnp
from jax import lax
from jax.sharding import PartitionSpec as P

MODEL_WIDTH = 8192
QUERY_HEADS = 64
KEY_VALUE_HEADS = 8
HEAD_SIZE = 128


beta_first = 0.9
beta_second = 0.999
correct_first = 0.9999734386011124
correct_second = 0.09520785288629038
adam_eps = 1e-08
learn_rate = 0.003
decay_rate = 0.1
norm_eps = 1e-06
rope_base = 1000000.0


def rotate(keys, positions):
    halfway = keys.shape[-1] // 2
    frequency = rope_base ** (-(jnp.arange(halfway, dtype=jnp.float32) * 2.0 / keys.shape[-1]))
    angles = positions[:, :, None] * frequency[None, None, :]
    cosine = jnp.cos(angles)[:, :, None, :]
    sine = jnp.sin(angles)[:, :, None, :]
    first_half = keys[..., :halfway]
    second_half = keys[..., halfway:]
    return jnp.concatenate(
        [first_half * cosine - second_half * sine, second_half * cosine + first_half * sine],
        axis=-1,
    )


def attention(queries, rotated_key_cache, head_value_cache, key_new, value_new, lengths):
    batch_rows, steps = (queries.shape[0], queries.shape[1])
    window = rotated_key_cache.shape[1]
    kv_heads = rotated_key_cache.shape[2] // HEAD_SIZE
    sharing_factor = QUERY_HEADS // KEY_VALUE_HEADS
    factor = HEAD_SIZE ** (-0.5)
    query_heads = queries.reshape(batch_rows, steps, kv_heads, sharing_factor, HEAD_SIZE)
    cache_key_seeds = rotated_key_cache.reshape(batch_rows, window, kv_heads, HEAD_SIZE)
    cache_values = head_value_cache.reshape(batch_rows, window, kv_heads, HEAD_SIZE)
    scores_cached = (
        jnp.einsum(
            "rsxgd,rlxd->rxgsl", query_heads, cache_key_seeds, preferred_element_type=jnp.float32
        )
        * factor
    )
    scores_fresh = (
        jnp.einsum("rsxgd,ruxd->rxgsu", query_heads, key_new, preferred_element_type=jnp.float32)
        * factor
    )
    present = (jnp.arange(window, dtype=jnp.int32)[None, :] < lengths[:, None])[
        :, None, None, None, :
    ]
    causal = (
        jnp.arange(steps, dtype=jnp.int32)[None, :] <= jnp.arange(steps, dtype=jnp.int32)[:, None]
    )[None, None, None, :, :]
    scores_cached = jnp.where(present, scores_cached, -jnp.inf)
    scores_fresh = jnp.where(causal, scores_fresh, -jnp.inf)
    ceiling = jnp.maximum(
        jnp.max(scores_cached, axis=-1, keepdims=True),
        jnp.max(scores_fresh, axis=-1, keepdims=True),
    )
    probs_cached = jnp.exp(scores_cached - ceiling)
    probs_fresh = jnp.exp(scores_fresh - ceiling)
    denom = jnp.sum(probs_cached, axis=-1, keepdims=True) + jnp.sum(
        probs_fresh, axis=-1, keepdims=True
    )
    weights_cached = probs_cached.astype(jnp.bfloat16)
    weights_fresh = probs_fresh.astype(jnp.bfloat16)
    blended = jnp.einsum(
        "rxgsl,rlxd->rsxgd", weights_cached, cache_values, preferred_element_type=jnp.float32
    )
    blended = blended + jnp.einsum(
        "rxgsu,ruxd->rsxgd", weights_fresh, value_new, preferred_element_type=jnp.float32
    )
    blended = blended / jnp.transpose(denom, (0, 3, 1, 2, 4))
    return blended.astype(jnp.bfloat16).reshape(
        batch_rows, steps, kv_heads * sharing_factor * HEAD_SIZE
    )


def shards(
    tokens,
    norm_gain,
    queries,
    rotated_key_cache,
    head_value_cache,
    lengths,
    master,
    moment_first,
    moment_second,
    gradient,
):
    average = beta_first * moment_first + (1.0 - beta_first) * gradient
    variance = beta_second * moment_second + (1.0 - beta_second) * gradient * gradient
    update = average / correct_first / (jnp.sqrt(variance / correct_second) + adam_eps)
    renewed = master - learn_rate * (update + decay_rate * master)
    layer_half = renewed.astype(jnp.bfloat16)
    widened, gain_whole = (
        lax.all_gather(tokens, ("tp", "fs"), axis=2, tiled=True),
        lax.all_gather(norm_gain, ("tp", "fs"), axis=0, tiled=True),
    )
    mean_square = (
        jnp.einsum("rsd,rsd->rs", widened, widened, preferred_element_type=jnp.float32)[..., None]
        / MODEL_WIDTH
    )
    normed = (widened * lax.rsqrt(mean_square + norm_eps) * gain_whole.astype(jnp.float32)).astype(
        jnp.bfloat16
    )
    batch_rows, steps = (tokens.shape[0], tokens.shape[1])
    flattened = normed.reshape(batch_rows * steps, MODEL_WIDTH)
    columns = layer_half.shape[1]
    gathered = lax.all_gather(layer_half, "grp", axis=0, tiled=True)
    projected_output = jnp.dot(flattened, gathered, preferred_element_type=jnp.float32)
    kv_heads = columns // (2 * HEAD_SIZE)
    projected_output = projected_output.reshape(batch_rows, steps, kv_heads, 2, HEAD_SIZE)
    positions = (lengths[:, None] + jnp.arange(steps, dtype=jnp.int32)[None, :]).astype(jnp.float32)
    key_new = rotate(projected_output[:, :, :, 0, :], positions).astype(jnp.bfloat16)
    value_new = projected_output[:, :, :, 1, :].astype(jnp.bfloat16)
    appended = jnp.stack([key_new, value_new], axis=3).reshape(batch_rows, steps, columns)
    attended = attention(queries, rotated_key_cache, head_value_cache, key_new, value_new, lengths)
    return (attended, appended, renewed, average, variance)


def solution(mesh):
    in_specs = (
        P("grp", None, ("tp", "fs")),
        P(("tp", "fs")),
        P("grp", None, ("tp", "fs")),
        P("grp", None, ("tp", "fs")),
        P("grp", None, ("tp", "fs")),
        P("grp"),
        P("grp", ("tp", "fs")),
        P("grp", ("tp", "fs")),
        P("grp", ("tp", "fs")),
        P("grp", ("tp", "fs")),
    )
    out_specs = (
        P("grp", None, ("tp", "fs")),
        P("grp", None, ("tp", "fs")),
        P("grp", ("tp", "fs")),
        P("grp", ("tp", "fs")),
        P("grp", ("tp", "fs")),
    )
    return jax.shard_map(shards, mesh=mesh, in_specs=in_specs, out_specs=out_specs, check_vma=False)
```

profile of v0, /device:TPU:2, one launch (start us, length us, event | category | flops | bytes accessed | tf_op | source)
XLA Modules:
  0.0 218.0 jit_solution(13725057092368029306)
XLA Ops:
  7.2 0.0 all-gather.3.cloned.1.call-start
  7.2 0.7 all-gather.3.cloned.1.call-update
  7.9 0.0 copy-start.6
  7.9 0.0 copy-start.1
  7.9 0.0 all-gather.5.cloned.1.call-start
  8.0 7.8 %fusion.33 = (bf16[1024,512]{1,0:T(8,128)(2,1)}, f32[1024,512]{1,0:T(8,128)}, f32[1024,512]{1,0:T(8,128)}, f32[1024,512]{1,0:T(8,128)}) fusion(f32[1024,512]{1,0:T(8,128)} %param.16, f32[1024,512]{1,0:T(8,128)} %param.19, f32[1024,512]{1,0:T(8,128)} %param.17, f32[1024,512]{1,0:T(8,128)} %param.18), kind=kLoop, calls=%fused_computation.56 | loop fusion | flops 8388608 | bytes 15728640 | tf_op jit(solution)/shard_map/convert_element_type | solution.py:103
  15.8 0.0 copy-start.2
  15.8 0.0 all-gather.5.cloned.1.call-update
  15.8 0.0 copy-done.6
  15.8 9.9 %all_gather.10 = bf16[8192]{0:T(1024)(128)(2,1)S(1)} all-gather(bf16[2048]{0:T(1024)(128)(2,1)S(1)} %copy-done.6), channel_id=1, replica_groups=mesh['grp'=8,'tp'=2,'fs'=2] {'tp','fs'}, dimensions={0}, use_global_device_ids=true | all-gather | bytes 20480 | tf_op jit(solution)/shard_map/all_gather | solution.py:106
  25.8 0.0 copy-done.1
  25.8 0.0 copy-start.3
  25.8 1.5 reshape.145
  27.3 0.0 copy-done.2
  27.3 0.0 copy-start.7
  27.3 1.1 reshape.144
  28.4 0.0 copy-done.3
  28.4 1.1 reshape.146
  29.5 0.0 copy-done.7
  29.5 0.1 iota_compare_fusion
  29.6 0.5 multiply_cosine_fusion
  30.1 2.4 %bitcast_reduce_fusion = (f32[64,2,8,4]{2,3,1,0:T(4,128)S(1)}, f32[64,2,32,4,8]{2,4,3,1,0:T(8,128)S(1)}) fusion(pred[64,32]{1,0:T(8,128)(4,1)S(1)} %iota_compare_fusion, bf16[64,4,2,8,128]{4,3,2,1,0:T(8,128)(2,1)} %reshape.145, bf16[64,32,2,128,1]{3,2,1,0,4:T(2,128)(2,1)} %bitcast.58), kind=kOutput, calls=%fused_computation.14 | convolution fusion | flops 33943552 | bytes 2639872 | tf_op jit(solution)/shard_map/rsxgd,rlxd->rxgsl/dot_general | solution.py:47
  32.5 11.8 %all-gather.3.cloned.1.call-done = bf16[64,4,8192]{2,1,0:T(4,128)(2,1)} async-done(((bf16[64,4,2048]{2,1,0:T(4,128)(2,1)}), bf16[64,4,8192]{2,1,0:T(4,128)(2,1)}) %all-gather.3.cloned.1.call-update) | async-done | bytes 4194320 | tf_op jit(solution)/shard_map/all_gather | solution.py:105
  44.3 0.0 copy-start
  44.4 4.6 %fusion.2 = f32[64,4]{1,0:T(8,128)S(1)} fusion(bf16[64,4,8192]{2,1,0:T(4,128)(2,1)} %all-gather.3.cloned.1.call-done), kind=kLoop, calls=%fused_computation.4 | loop fusion | flops 6291200 | bytes 4195328 | tf_op jit(solution)/shard_map/rsd,rsd->rs/dot_general | solution.py:109
  49.0 0.0 copy-done
  49.0 4.7 %fusion.3 = bf16[64,4,8192,1,1]{2,1,0,4,3:T(4,128)(2,1)} fusion(bf16[64,4,8192]{2,1,0:T(4,128)(2,1)S(1)} %copy-done, f32[8192]{0:T(1024)S(1)} %convert_element_type.44, f32[64,4]{1,0:T(8,128)S(1)} %add_rsqrt_fusion), kind=kLoop, calls=%fused_computation.5 | loop fusion | flops 8388608 | bytes 8422400 | tf_op jit(solution)/shard_map/convert_element_type | solution.py:112
  53.7 118.4 %all-gather.5.cloned.1.call-done = bf16[8192,512]{1,0:T(8,128)(2,1)} async-done(((bf16[1024,512]{1,0:T(8,128)(2,1)}), bf16[8192,512]{1,0:T(8,128)(2,1)}) %all-gather.5.cloned.1.call-update) | async-done | bytes 8388624 | tf_op jit(solution)/shard_map/all_gather | solution.py:118
  172.1 11.9 %copy.41 = bf16[512,8192]{1,0:T(8,128)(2,1)} copy(bf16[512,8192]{0,1:T(8,128)(2,1)} %bitcast.53) | data formatting | bytes 16777216 | tf_op jit(solution)/shard_map/dot_general | solution.py:119
  184.0 13.5 %fusion.4 = f32[64,4,2,2,128]{4,0,3,2,1:T(8,128)S(1)} fusion(bf16[2,2,128,8192,1]{3,2,1,0,4:T(8,128)(2,1)} %bitcast.54, bf16[64,4,8192,1,1]{2,1,0,4,3:T(4,128)(2,1)} %fusion.3), kind=kOutput, calls=%fused_computation.6 | convolution fusion | flops 2147483648 | bytes 13107200 | tf_op jit(solution)/shard_map/dot_general | solution.py:119
  197.5 0.0 copy-start.5
  197.6 0.2 subtract_convert_fusion
  197.8 0.1 maximum_bitcast_fusion
  197.9 0.9 copy-done.5
  198.8 4.7 %fusion.35 = (f32[64,2,8,4]{2,3,1,0:T(4,128)S(1)}, f32[64,2,8,4,4]{2,4,3,1,0:T(4,128)S(1)}) fusion(bf16[64,4,2,8,128]{4,3,2,1,0:T(8,128)(2,1)S(1)} %copy-done.5, bf16[64,4,2,128,1]{3,0,2,1,4:T(8,128)(2,1)S(1)} %maximum_bitcast_fusion, pred[4,4]{1,0:T(4,128)(4,1)S(1)} %iota_compare_fusion.1), kind=kOutput, calls=%fused_computation.57 | convolution fusion | flops 4239360 | bytes 1261584 | tf_op jit(solution)/shard_map/rsxgd,ruxd->rxgsu/dot_general | solution.py:53
  203.5 0.1 max.8
  203.6 0.0 copy-start.4
  203.6 1.0 fusion.25
  204.6 1.4 fusion.10
  206.0 0.0 copy-done.4
  206.0 1.4 fusion.14
  207.3 0.1 add_bitcast_fusion
  207.4 1.2 fusion.8
  208.6 0.2 copy.72
  208.8 1.1 reshape.157
  209.9 0.1 pad_maximum_fusion
  210.1 0.3 copy.73
  210.3 0.8 reshape.158
  (8 shorter events, 0.1 us)
Async XLA Ops:
  7.2 37.2 %all-gather.3.cloned.1.call-start = ((), (), s32[]{:S(2)}) async-start(), calls=%async_computation | async-start | bytes 5242880 | tf_op jit(solution)/shard_map/all_gather | solution.py:105
  7.9 7.9 %copy-start.6 = (bf16[2048]{0:T(1024)(128)(2,1)S(1)}, bf16[2048]{0:T(1024)(128)(2,1)}, u32[]{:S(2)}) copy-start(bf16[2048]{0:T(1024)(128)(2,1)} %param.11) | copy-start | bytes 12292
  7.9 17.8 %copy-start.1 = (bf16[64,4,2048]{2,1,0:T(4,128)(2,1)S(1)}, bf16[64,4,2048]{2,1,0:T(4,128)(2,1)}, u32[]{:S(2)}) copy-start(bf16[64,4,2048]{2,1,0:T(4,128)(2,1)} %param.12) | copy-start | bytes 3145732
  7.9 164.2 %all-gather.5.cloned.1.call-start = ((), (), s32[]{:S(2)}) async-start(), calls=%async_computation.1 | async-start | bytes 9437184 | tf_op jit(solution)/shard_map/all_gather | solution.py:118
  15.8 11.5 %copy-start.2 = (bf16[64,32,256]{2,1,0:T(8,128)(2,1)S(1)}, bf16[64,32,256]{2,1,0:T(8,128)(2,1)}, u32[]{:S(2)}) copy-start(bf16[64,32,256]{2,1,0:T(8,128)(2,1)} %param.13) | copy-start | bytes 3145732
  25.8 2.6 %copy-start.3 = (bf16[64,32,256]{2,1,0:T(8,128)(2,1)S(1)}, bf16[64,32,256]{2,1,0:T(8,128)(2,1)}, u32[]{:S(2)}) copy-start(bf16[64,32,256]{2,1,0:T(8,128)(2,1)} %param.14) | copy-start | bytes 3145732
  27.3 2.2 %copy-start.7 = (s32[64]{0:T(128)S(1)}, s32[64]{0:T(128)}, u32[]{:S(2)}) copy-start(s32[64]{0:T(128)} %param.15) | copy-start | bytes 772
  44.3 4.6 %copy-start = (bf16[64,4,8192]{2,1,0:T(4,128)(2,1)S(1)}, bf16[64,4,8192]{2,1,0:T(4,128)(2,1)}, u32[]{:S(2)}) copy-start(bf16[64,4,8192]{2,1,0:T(4,128)(2,1)} %all-gather.3.cloned.1.call-done) | copy-start | bytes 12582916
  197.5 1.2 copy-start.5
  203.6 2.4 %copy-start.4 = (bf16[64,32,2,128]{3,2,1,0:T(2,128)(2,1)S(1)}, bf16[64,32,2,128]{3,2,1,0:T(2,128)(2,1)}, u32[]{:S(2)}) copy-start(bf16[64,32,2,128]{3,2,1,0:T(2,128)(2,1)} %reshape.146) | copy-start | bytes 3145732
Sparse Core Ops, SparseCore 0:
  9.5 34.7 all-gather.2
  46.5 125.5 all-gather.4
where the time goes:
time: 220 us; the launch traced here: 218 us
  waiting for transfers between devices  131 us (60%)
  matrix products  23.2 us (11%)
  other arithmetic  20.7 us (9%)
  local copies, waits for them, and re-layouts  18.9 us (9%)
  between operations  14.2 us (6%)
  blocking collectives  9.93 us (5%)
    all_gather x1, waiting for transfers between devices, shards(): gathered = lax.all_gather(layer_half, 'grp', axis=0, tiled=True)  118 us
    dot_general x1, matrix products, shards(): jnp.dot(flattened, gathered, preferred_element_type=jnp.float32)  13.5 us
    dot_general x1, local copies, waits for them, and re-layouts, shards(): jnp.dot(flattened, gathered, preferred_element_type=jnp.float32)  11.9 us
    all_gather x1, waiting for transfers between devices, shards(): lax.all_gather(tokens, ('tp', 'fs'), axis=2, tiled=True)  11.8 us
    all_gather x1, blocking collectives, shards(): lax.all_gather(norm_gain, ('tp', 'fs'), axis=0, tiled=True)  9.93 us
    convert_element_type x1, other arithmetic, shards(): layer_half = renewed.astype(jnp.bfloat16)  7.82 us
    dot_general x1, matrix products, attention(): jnp.einsum('rsxgd,ruxd->rxgsu', query_heads, key_new, preferred_element_t...  4.73 us
    convert_element_type x1, other arithmetic, shards(): (widened * lax.rsqrt(mean_square + norm_eps) * gain_whole.astype(jnp.floa...  4.72 us
  transfers between devices with their start and end apart: 2, of which 2 were waited for; matrix products, arithmetic and copies ran while one was open for 11% of the time, Pallas kernels for 0%

commit v1 on v0

--- a/solution.py
+++ b/solution.py
@@ -1,7 +1,14 @@
+import functools
+
 import jax
 import jax.numpy as jnp
 from jax import lax
+from jax.experimental import pallas as pl
+from jax.experimental.pallas import tpu as pltpu
 from jax.sharding import PartitionSpec as P
+
+MESH_ID = pl.DeviceIdType.MESH
+PIECES = 2
 
 MODEL_WIDTH = 8192
 QUERY_HEADS = 64
@@ -84,7 +91,215 @@
     )
 
 
+def exchange_kernel(sizes, tok_ref, gain_ref, w_ref, o_ref, sent, held, squares, squares_in, pair_out, pair_in, total,
+                    line_out, line_in, sq_s, sq_r, tok_s, tok_r, fx_s, fc_s, pair_s, pair_r, line_s, line_r):
+    grp, tp, fs = sizes
+    line = grp // 2
+    g, t, f = lax.axis_index("grp"), lax.axis_index("tp"), lax.axis_index("fs")
+    z, y = g // 2, lax.rem(g, 2)
+    rows, width = tok_ref.shape
+    depth = w_ref.shape[0]
+    blocks = width // depth
+    piece = rows // PIECES
+    me = t * fs + f
+    owner = g // blocks
+    owner_t, owner_f = owner // fs, lax.rem(owner, fs)
+
+    def remote(src, dst, ss, rs, device):
+        return pltpu.make_async_remote_copy(
+            src_ref=src, dst_ref=dst, send_sem=ss, recv_sem=rs, device_id=device, device_id_type=MESH_ID
+        )
+
+    barrier = pltpu.get_barrier_semaphore()
+    peers = [(lax.rem(g + i, grp), t, f) for i in range(1, grp)]
+    mates = [(g, 1 - t, f), (g, t, 1 - f), (g, 1 - t, 1 - f)]
+    for device in peers + mates:
+        pl.semaphore_signal(barrier, inc=1, device_id=device, device_id_type=MESH_ID)
+
+    wide = tok_ref[...].astype(jnp.float32)
+    wide = wide * wide
+    part = wide[:, :128]
+    for i in range(1, width // 128):
+        part = part + wide[:, i * 128 : (i + 1) * 128]
+    squares[...] = jnp.broadcast_to(jnp.sum(part.T, axis=0, keepdims=True), squares.shape)
+    pl.semaphore_wait(barrier, len(peers) + len(mates))
+    sq = [remote(squares, squares_in.at[i], sq_s.at[i], sq_r.at[i], mates[i]) for i in range(3)]
+    for copy in sq:
+        copy.start()
+    for copy in sq:
+        copy.wait()
+    summed = (squares[...] + squares_in[0]) + (squares_in[1] + squares_in[2])
+    scale = lax.rsqrt(summed / (width * tp * fs) + norm_eps)
+    scale = jnp.broadcast_to(scale[0:1], (128, rows)).T[:, :1]
+
+    for c in range(PIECES):
+        window = pl.ds(c * piece, piece)
+        for j in range(blocks):
+            cols = pl.ds(j * depth, depth)
+            sent[j, window, :] = (
+                tok_ref[window, cols].astype(jnp.float32)
+                * scale[c * piece : (c + 1) * piece]
+                * gain_ref[:, cols].astype(jnp.float32)
+            ).astype(jnp.bfloat16)
+        for j in range(blocks):
+            dest = me * blocks + j
+
+            @pl.when(dest != g)
+            def _(c=c, j=j, dest=dest, window=window):
+                remote(sent.at[j, window], held.at[g, window], tok_s.at[j, c], tok_r.at[g, c], (dest, t, f)).start()
+
+            @pl.when(dest == g)
+            def _(c=c, j=j, window=window):
+                pltpu.make_async_copy(sent.at[j, window], held.at[g, window], tok_r.at[g, c]).start()
+
+    def order(i):
+        return [0, *[d for k in range(1, line) for d in ((k, line - k) if k < line - k else (k,)) if k <= line - k]][i]
+
+    def forward(slot, window, k, c, end):
+        across = remote(held.at[slot, window], held.at[slot, window], fx_s.at[k, c], tok_r.at[slot, c], mates[1])
+        beside = remote(held.at[slot, window], held.at[slot, window], fc_s.at[k, c], tok_r.at[slot, c], mates[0])
+
+        @pl.when((t == owner_t) & (f == owner_f))
+        def _():
+            across.wait_send() if end else across.start()
+
+        @pl.when(t == owner_t)
+        def _():
+            beside.wait_send() if end else beside.start()
+
+    def pair_copy(i):
+        return remote(pair_out.at[i], pair_in.at[i], pair_s.at[i], pair_r.at[i], (z * 2 + 1 - y, t, f))
+
+    def line_copy(i):
+        return remote(
+            line_out.at[i], line_in.at[i], line_s.at[i], line_r.at[i], (lax.rem(z + order(i), line) * 2 + y, t, f)
+        )
+
+    def combine(i):
+        pair_copy(i).wait_recv()
+        both = total[i] + pair_in[i].astype(jnp.float32)
+        if i == 0:
+            total[0] = both
+        else:
+            line_out[i] = both.astype(jnp.bfloat16)
+            line_copy(i).start()
+
+    for i in range(line):
+        zs = lax.rem(z + order(i), line)
+        for k, slot in enumerate((zs * 2 + 1 - y, zs * 2 + y)):
+            for c in range(PIECES):
+                window = pl.ds(c * piece, piece)
+                remote(
+                    held.at[slot, window], held.at[slot, window], fx_s.at[0, 0], tok_r.at[slot, c], mates[1]
+                ).wait_recv()
+                forward(slot, window, 2 * i + k, c, False)
+            product = jnp.dot(held[slot], w_ref[...], preferred_element_type=jnp.float32)
+            if k == 0:
+                pair_out[i] = product.astype(jnp.bfloat16)
+                pair_copy(i).start()
+            else:
+                total[i] = product
+        if i > 0:
+            combine(i - 1)
+    combine(line - 1)
+    result = total[0]
+    for i in range(1, line):
+        line_copy(i).wait_recv()
+        result = result + line_in[i].astype(jnp.float32)
+    o_ref[...] = result
+
+    for c in range(PIECES):
+        window = pl.ds(c * piece, piece)
+        for j in range(blocks):
+            dest = me * blocks + j
+
+            @pl.when(dest != g)
+            def _(c=c, j=j, dest=dest, window=window):
+                remote(
+                    sent.at[j, window], held.at[g, window], tok_s.at[j, c], tok_r.at[g, c], (dest, t, f)
+                ).wait_send()
+
+    for i in range(line):
+        zs = lax.rem(z + order(i), line)
+        for k, slot in enumerate((zs * 2 + 1 - y, zs * 2 + y)):
+            for c in range(PIECES):
+                forward(slot, pl.ds(c * piece, piece), 2 * i + k, c, True)
+        pair_copy(i).wait_send()
+        if i > 0:
+            line_copy(i).wait_send()
+
+
+def exchange(sizes, tokens, gain, layer):
+    grp, _, _ = sizes
+    rows, width = tokens.shape
+    depth, columns = layer.shape
+    blocks, line = width // depth, grp // 2
+    dma = pltpu.SemaphoreType.DMA
+    vmem = pl.BlockSpec(memory_space=pltpu.VMEM)
+    return pl.pallas_call(
+        functools.partial(exchange_kernel, sizes),
+        out_shape=jax.ShapeDtypeStruct((rows, columns), jnp.float32),
+        in_specs=[vmem] * 3,
+        out_specs=vmem,
+        scratch_shapes=[
+            pltpu.VMEM((blocks, rows, depth), jnp.bfloat16),
+            pltpu.VMEM((grp, rows, depth), jnp.bfloat16),
+            pltpu.VMEM((8, rows), jnp.float32),
+            pltpu.VMEM((3, 8, rows), jnp.float32),
+            pltpu.VMEM((line, rows, columns), jnp.bfloat16),
+            pltpu.VMEM((line, rows, columns), jnp.bfloat16),
+            pltpu.VMEM((line, rows, columns), jnp.float32),
+            pltpu.VMEM((line, rows, columns), jnp.bfloat16),
+            pltpu.VMEM((line, rows, columns), jnp.bfloat16),
+            dma((3,)),
+            dma((3,)),
+            dma((blocks, PIECES)),
+            dma((grp, PIECES)),
+            dma((grp, PIECES)),
+            dma((grp, PIECES)),
+            dma((line,)),
+            dma((line,)),
+            dma((line,)),
+            dma((line,)),
+        ],
+        compiler_params=pltpu.CompilerParams(collective_id=0, has_side_effects=True, vmem_limit_bytes=48 << 20),
+    )(tokens, gain, layer)
+
+
+def project(sizes, tokens, norm_gain, layer_half):
+    batch_rows, steps, width = tokens.shape
+    return exchange(sizes, tokens.reshape(batch_rows * steps, width), norm_gain.reshape(1, width), layer_half)
+
+
+def fits(sizes, tokens, layer_half):
+    grp, tp, fs = sizes
+    rows, width, depth = tokens.shape[0] * tokens.shape[1], tokens.shape[2], layer_half.shape[0]
+    return (
+        tp == 2 and fs == 2 and grp % 2 == 0 and 4 <= grp <= 16 and depth % 128 == 0 and width % depth == 0
+        and rows % (128 * PIECES) == 0 and layer_half.shape[1] % 128 == 0
+    )
+
+
+def project_gathered(tokens, norm_gain, layer_half):
+    batch_rows, steps = (tokens.shape[0], tokens.shape[1])
+    widened, gain_whole = (
+        lax.all_gather(tokens, ("tp", "fs"), axis=2, tiled=True),
+        lax.all_gather(norm_gain, ("tp", "fs"), axis=0, tiled=True),
+    )
+    mean_square = (
+        jnp.einsum("rsd,rsd->rs", widened, widened, preferred_element_type=jnp.float32)[..., None]
+        / MODEL_WIDTH
+    )
+    normed = (widened * lax.rsqrt(mean_square + norm_eps) * gain_whole.astype(jnp.float32)).astype(
+        jnp.bfloat16
+    )
+    flattened = normed.reshape(batch_rows * steps, MODEL_WIDTH)
+    gathered = lax.all_gather(layer_half, "grp", axis=0, tiled=True)
+    return jnp.dot(flattened, gathered, preferred_element_type=jnp.float32)
+
+
 def shards(
+    sizes,
     tokens,
     norm_gain,
     queries,
@@ -101,22 +316,12 @@
     update = average / correct_first / (jnp.sqrt(variance / correct_second) + adam_eps)
     renewed = master - learn_rate * (update + decay_rate * master)
     layer_half = renewed.astype(jnp.bfloat16)
-    widened, gain_whole = (
-        lax.all_gather(tokens, ("tp", "fs"), axis=2, tiled=True),
-        lax.all_gather(norm_gain, ("tp", "fs"), axis=0, tiled=True),
-    )
-    mean_square = (
-        jnp.einsum("rsd,rsd->rs", widened, widened, preferred_element_type=jnp.float32)[..., None]
-        / MODEL_WIDTH
-    )
-    normed = (widened * lax.rsqrt(mean_square + norm_eps) * gain_whole.astype(jnp.float32)).astype(
-        jnp.bfloat16
-    )
     batch_rows, steps = (tokens.shape[0], tokens.shape[1])
-    flattened = normed.reshape(batch_rows * steps, MODEL_WIDTH)
     columns = layer_half.shape[1]
-    gathered = lax.all_gather(layer_half, "grp", axis=0, tiled=True)
-    projected_output = jnp.dot(flattened, gathered, preferred_element_type=jnp.float32)
+    if fits(sizes, tokens, layer_half):
+        projected_output = project(sizes, tokens, norm_gain, layer_half)
+    else:
+        projected_output = project_gathered(tokens, norm_gain, layer_half)
     kv_heads = columns // (2 * HEAD_SIZE)
     projected_output = projected_output.reshape(batch_rows, steps, kv_heads, 2, HEAD_SIZE)
     positions = (lengths[:, None] + jnp.arange(steps, dtype=jnp.int32)[None, :]).astype(jnp.float32)
@@ -147,4 +352,6 @@
         P("grp", ("tp", "fs")),
         P("grp", ("tp", "fs")),
     )
-    return jax.shard_map(shards, mesh=mesh, in_specs=in_specs, out_specs=out_specs, check_vma=False)
+    return jax.shard_map(
+        functools.partial(shards, tuple(mesh.shape[name] for name in ("grp", "tp", "fs"))), mesh=mesh, in_specs=in_specs, out_specs=out_specs, check_vma=False,
+    )

time: 220 us -> 124 us (0.56)
  waiting for transfers between devices: 131 us -> 0 us
  Pallas kernels: 0 us -> 91.4 us
  between operations: 14.2 us -> 0.93 us
  matrix products: 23.2 us -> 10.7 us
  local copies, waits for them, and re-layouts: 18.9 us -> 8.85 us
  blocking collectives: 9.93 us -> 0 us
  other arithmetic: 20.7 us -> 11.9 us
    all_gather x2 -> x0, waiting for transfers between devices: 130 us -> none  [the longest x1 118 us: shards(): gathered = lax.all_gather(layer_half, 'grp', axis=0, tiled=True)]
    pallas_call x0 -> x1, Pallas kernels: none -> 91.4 us  [exchange(): pl.pallas_call(functools.partial(exchange_kernel, sizes), out_shape=jax.S...]
    dot_general x1 -> x0, matrix products: 13.5 us -> none  [shards(): jnp.dot(flattened, gathered, preferred_element_type=jnp.float32)]
    dot_general x1 -> x0, local copies, waits for them, and re-layouts: 11.9 us -> none  [shards(): jnp.dot(flattened, gathered, preferred_element_type=jnp.float32)]
    all_gather x1 -> x0, blocking collectives: 9.93 us -> none  [shards(): lax.all_gather(norm_gain, ('tp', 'fs'), axis=0, tiled=True)]
    convert_element_type x2 -> x0, other arithmetic: 4.73 us -> none  [the longest x1 4.72 us: shards(): (widened * lax.rsqrt(mean_square + norm_eps) * gain_whole.astype(jnp.floa...]
    dot_general x1 -> x0, other arithmetic: 4.59 us -> none  [shards(): jnp.einsum('rsd,rsd->rs', widened, widened, preferred_element_type=jnp.fl...]
  transfers between devices with their start and end apart: 2 -> 0, of which waited for: 2 -> 0; matrix products, arithmetic and copies ran while one was open for 11% -> 0% of each run, Pallas kernels for 0% -> 0%
where the time goes in v1:
time: 124 us
  Pallas kernels  91.4 us (74%)
  other arithmetic  11.9 us (10%)
  matrix products  10.7 us (9%)
  local copies, waits for them, and re-layouts  8.85 us (7%)
    pallas_call x1, Pallas kernels, exchange(): pl.pallas_call(functools.partial(exchange_kernel, sizes), out_shape=jax.S...  91.4 us
    convert_element_type x1, other arithmetic, shards(): layer_half = renewed.astype(jnp.bfloat16)  6.74 us
    dot_general x1, matrix products, attention(): jnp.einsum('rsxgd,ruxd->rxgsu', query_heads, key_new, preferred_element_t...  4.8 us
    dot_general x1, matrix products, attention(): jnp.einsum('rsxgd,rlxd->rxgsl', query_heads, cache_key_seeds, preferred_e...  3.39 us
    unnamed x24, local copies, waits for them, and re-layouts  2.55 us

profile of v1, /device:TPU:2, one launch (start us, length us, event | category | flops | bytes accessed | tf_op | source)
XLA Modules:
  0.0 123.7 jit_solution(11409128045541288052)
XLA Ops:
  0.6 0.0 copy-start.2
  0.6 0.8 iota_compare_fusion
  1.5 1.7 %reshape.144 = bf16[64,4,2,8,128]{4,3,2,1,0:T(8,128)(2,1)S(1)} reshape(bf16[64,4,2048]{2,1,0:T(4,128)(2,1)} %param.12) | data formatting | bytes 2097152 | tf_op jit(solution)/shard_map/reshape | solution.py:50
  3.2 0.0 copy-done.2
  3.2 0.0 copy-start.4
  3.2 1.3 %reshape.143 = bf16[64,32,2,128]{3,2,1,0:T(2,128)(2,1)} reshape(bf16[64,32,256]{2,1,0:T(8,128)(2,1)S(1)} %copy-done.2) | data formatting | bytes 2097152 | tf_op jit(solution)/shard_map/reshape | solution.py:51
  4.5 0.0 copy-start.3
  4.5 3.4 %bitcast_reduce_fusion = (f32[64,2,8,4]{2,3,1,0:T(4,128)S(1)}, f32[64,2,32,4,8]{2,4,3,1,0:T(8,128)}) fusion(pred[64,32]{1,0:T(8,128)(4,1)S(1)} %iota_compare_fusion, bf16[64,4,2,8,128]{4,3,2,1,0:T(8,128)(2,1)S(1)} %reshape.144, bf16[64,32,2,128,1]{3,2,1,0,4:T(2,128)(2,1)} %bitcast.52), kind=kOutput, calls=%fused_computation.6 | convolution fusion | flops 33943552 | bytes 2639872 | tf_op jit(solution)/shard_map/rsxgd,rlxd->rxgsl/dot_general | solution.py:54
  7.9 0.0 copy-done.4
  7.9 0.0 copy-done.3
  8.0 0.0 copy-start.7
  8.0 0.0 copy-start
  8.0 1.1 reshape.148
  9.1 1.3 %reshape.145.tok_ref = bf16[256,2048]{1,0:T(8,128)(2,1)S(1)} reshape(bf16[64,4,2048]{2,1,0:T(4,128)(2,1)} %param.10) | data formatting | bytes 2097152 | tf_op jit(solution)/shard_map/reshape | solution.py:271
  10.4 0.0 copy-done.7
  10.5 0.0 copy-done
  10.5 6.7 %fusion.29 = (bf16[1024,512]{1,0:T(8,128)(2,1)S(1)}, f32[1024,512]{1,0:T(8,128)}, f32[1024,512]{1,0:T(8,128)}, f32[1024,512]{1,0:T(8,128)}) fusion(f32[1024,512]{1,0:T(8,128)S(1)} %copy-done, f32[1024,512]{1,0:T(8,128)} %param.19, f32[1024,512]{1,0:T(8,128)} %param.17, f32[1024,512]{1,0:T(8,128)} %param.18), kind=kLoop, calls=%fused_computation.49 | loop fusion | flops 8388608 | bytes 15728640 | tf_op jit(solution)/shard_map/convert_element_type | solution.py:318
  17.2 0.0 copy-start.8
  17.2 91.4 %shard_map.137 = f32[256,512]{1,0:T(8,128)S(1)} custom-call(bf16[256,2048]{1,0:T(8,128)(2,1)S(1)} %reshape.145.tok_ref, bf16[1,2048]{1,0:T(2,128)(2,1)S(1)} %reshape.146.gain_ref, bf16[1024,512]{1,0:T(8,128)(2,1)S(1)} %get-tuple-element.10.w_ref), custom_call_target="tpu_custom_call" | custom-call | tf_op jit(solution)/shard_map/pallas_call | solution.py:239
  108.6 0.0 copy-start.5
  108.6 0.3 reshape.147
  109.0 0.2 slice.16
  109.1 0.1 copy.62
  109.2 0.0 copy-done.8
  109.3 0.1 add_convert_fusion.1
  109.3 1.2 multiply_cosine_fusion
  110.6 0.2 subtract_convert_fusion
  110.8 0.0 copy-done.5
  110.8 0.0 copy-start.1
  110.8 0.0 copy-start.6
  110.8 4.8 %fusion.31 = (f32[64,2,8,4]{2,3,1,0:T(4,128)S(1)}, f32[64,2,8,4,4]{2,4,3,1,0:T(4,128)S(1)}) fusion(bf16[64,4,2,8,128]{4,3,2,1,0:T(8,128)(2,1)S(1)} %copy-done.5, bf16[64,4,2,64]{3,1,2,0:T(4,128)(2,1)S(1)} %get-tuple-element.15, bf16[64,4,2,64]{3,1,2,0:T(4,128)(2,1)S(1)} %get-tuple-element.14, pred[4,4]{1,0:T(4,128)(4,1)S(1)} %iota_compare_fusion.1), kind=kOutput, calls=%fused_computation.50 | convolution fusion | flops 4501504 | bytes 1261584 | tf_op jit(solution)/shard_map/rsxgd,ruxd->rxgsu/dot_general | solution.py:60
  115.6 0.1 max.8
  115.7 0.0 copy-done.1
  115.7 0.0 copy-done.6
  115.7 1.3 %fusion.8 = f32[64,2,8,4,128]{4,2,3,1,0:T(8,128)S(1)} fusion(f32[64,2,32,4,8]{2,4,3,1,0:T(8,128)S(1)} %copy-done.1, bf16[64,32,2,128,1]{3,2,1,0,4:T(2,128)(2,1)S(1)} %bitcast.51, f32[64,2,8,4]{2,3,1,0:T(4,128)S(1)} %max.8, pred[64,32]{1,0:T(8,128)(4,1)S(1)} %iota_compare_fusion), kind=kOutput, calls=%fused_computation.16 | convolution fusion | flops 34078720 | bytes 3688448 | tf_op jit(solution)/shard_map/rxgsl,rlxd->rsxgd/dot_general | solution.py:82
  117.1 1.4 %fusion.4 = f32[64,2,8,4]{2,3,1,0:T(4,128)S(1)} fusion(f32[64,2,32,4,8]{2,4,3,1,0:T(8,128)S(1)} %copy-done.1, f32[64,2,8,4]{2,3,1,0:T(4,128)S(1)} %max.8, pred[64,32]{1,0:T(8,128)(4,1)S(1)} %iota_compare_fusion), kind=kLoop, calls=%fused_computation.11 | loop fusion | flops 520192 | bytes 559104 | tf_op jit(solution)/shard_map/reduce_sum | solution.py:77
  118.5 1.0 fusion.19
  119.5 0.1 add_bitcast_fusion
  119.5 0.3 slice.19
  119.8 0.1 copy.55
  119.9 1.2 fusion.2
  121.1 0.2 copy.39
  121.3 1.1 reshape.155
  122.4 0.2 pad_maximum_fusion
  122.6 0.3 copy.40
  122.9 0.8 reshape.156
  (3 shorter events, 0.0 us)
Async XLA Ops:
  0.6 2.6 %copy-start.2 = (bf16[64,32,256]{2,1,0:T(8,128)(2,1)S(1)}, bf16[64,32,256]{2,1,0:T(8,128)(2,1)}, u32[]{:S(2)}) copy-start(bf16[64,32,256]{2,1,0:T(8,128)(2,1)} %param.13) | copy-start | bytes 3145732
  3.2 4.7 %copy-start.4 = (bf16[64,4,2,8,128]{4,3,2,1,0:T(8,128)(2,1)}, bf16[64,4,2,8,128]{4,3,2,1,0:T(8,128)(2,1)S(1)}, u32[]{:S(2)}) copy-start(bf16[64,4,2,8,128]{4,3,2,1,0:T(8,128)(2,1)S(1)} %reshape.144) | copy-start | bytes 3145732
  4.5 3.4 %copy-start.3 = (bf16[64,32,256]{2,1,0:T(8,128)(2,1)S(1)}, bf16[64,32,256]{2,1,0:T(8,128)(2,1)}, u32[]{:S(2)}) copy-start(bf16[64,32,256]{2,1,0:T(8,128)(2,1)} %param.14) | copy-start | bytes 3145732
  8.0 2.5 %copy-start.7 = (bf16[2048]{0:T(1024)(128)(2,1)S(1)}, bf16[2048]{0:T(1024)(128)(2,1)}, u32[]{:S(2)}) copy-start(bf16[2048]{0:T(1024)(128)(2,1)} %param.11) | copy-start | bytes 12292
  8.0 2.5 %copy-start = (f32[1024,512]{1,0:T(8,128)S(1)}, f32[1024,512]{1,0:T(8,128)}, u32[]{:S(2)}) copy-start(f32[1024,512]{1,0:T(8,128)} %param.16) | copy-start | bytes 6291460
  17.2 92.0 %copy-start.8 = (s32[64]{0:T(128)S(1)}, s32[64]{0:T(128)}, u32[]{:S(2)}) copy-start(s32[64]{0:T(128)} %param.15) | copy-start | bytes 772
  108.6 2.2 %copy-start.5 = (bf16[64,4,2,8,128]{4,3,2,1,0:T(8,128)(2,1)S(1)}, bf16[64,4,2,8,128]{4,3,2,1,0:T(8,128)(2,1)}, u32[]{:S(2)}) copy-start(bf16[64,4,2,8,128]{4,3,2,1,0:T(8,128)(2,1)} %copy-done.4) | copy-start | bytes 3145732
  110.8 4.9 %copy-start.1 = (f32[64,2,32,4,8]{2,4,3,1,0:T(8,128)S(1)}, f32[64,2,32,4,8]{2,4,3,1,0:T(8,128)}, u32[]{:S(2)}) copy-start(f32[64,2,32,4,8]{2,4,3,1,0:T(8,128)} %get-tuple-element.19) | copy-start | bytes 1572868
  110.8 4.9 %copy-start.6 = (bf16[64,32,2,128]{3,2,1,0:T(2,128)(2,1)S(1)}, bf16[64,32,2,128]{3,2,1,0:T(2,128)(2,1)}, u32[]{:S(2)}) copy-start(bf16[64,32,2,128]{3,2,1,0:T(2,128)(2,1)} %reshape.148) | copy-start | bytes 3145732

commit v2 on v1

--- a/solution.py
+++ b/solution.py
@@ -8,7 +8,7 @@
 from jax.sharding import PartitionSpec as P
 
 MESH_ID = pl.DeviceIdType.MESH
-PIECES = 2
+PIECES = 4
 
 MODEL_WIDTH = 8192
 QUERY_HEADS = 64
@@ -91,8 +91,10 @@
     )
 
 
-def exchange_kernel(sizes, tok_ref, gain_ref, w_ref, o_ref, sent, held, squares, squares_in, pair_out, pair_in, total,
-                    line_out, line_in, sq_s, sq_r, tok_s, tok_r, fx_s, fc_s, pair_s, pair_r, line_s, line_r):
+def exchange_kernel(sizes, tok_ref, gain_ref, w_ref, cos_ref, sin_ref, present_ref, q_hbm, k_hbm, v_hbm, out_ref, app_ref,
+                    sent, held, squares, squares_in, pair_out, pair_in, total, line_out, line_in, q_ref, k_ref, v_ref,
+                    part_out, part_max, part_sum, sq_s, sq_r, tok_s, tok_r, fx_s, fc_s, side_s, pair_s, pair_r, line_s, line_r,
+                    load_s):
     grp, tp, fs = sizes
     line = grp // 2
     g, t, f = lax.axis_index("grp"), lax.axis_index("tp"), lax.axis_index("fs")
@@ -113,7 +115,15 @@
     barrier = pltpu.get_barrier_semaphore()
     peers = [(lax.rem(g + i, grp), t, f) for i in range(1, grp)]
     mates = [(g, 1 - t, f), (g, t, 1 - f), (g, 1 - t, 1 - f)]
-    for device in peers + mates:
+    beside_z = z + 1 - 2 * lax.rem(z, 2)
+    sides = [(beside_z * 2 + i, t, 1 - f) for i in range(2)]
+    loads = [
+        pltpu.make_async_copy(src, dst, load_s.at[i])
+        for i, (src, dst) in enumerate(((q_hbm, q_ref), (k_hbm, k_ref), (v_hbm, v_ref)))
+    ]
+    for copy in loads:
+        copy.start()
+    for device in peers + mates + sides:
         pl.semaphore_signal(barrier, inc=1, device_id=device, device_id_type=MESH_ID)
 
     wide = tok_ref[...].astype(jnp.float32)
@@ -122,7 +132,7 @@
     for i in range(1, width // 128):
         part = part + wide[:, i * 128 : (i + 1) * 128]
     squares[...] = jnp.broadcast_to(jnp.sum(part.T, axis=0, keepdims=True), squares.shape)
-    pl.semaphore_wait(barrier, len(peers) + len(mates))
+    pl.semaphore_wait(barrier, len(peers) + len(mates) + len(sides))
     sq = [remote(squares, squares_in.at[i], sq_s.at[i], sq_r.at[i], mates[i]) for i in range(3)]
     for copy in sq:
         copy.start()
@@ -132,6 +142,27 @@
     scale = lax.rsqrt(summed / (width * tp * fs) + norm_eps)
     scale = jnp.broadcast_to(scale[0:1], (128, rows)).T[:, :1]
 
+    def send_block(c, j, end):
+        dest = me * blocks + j
+        window = pl.ds(c * piece, piece)
+        src, dst = sent.at[j, window], held.at[g, window]
+        away = remote(src, dst, tok_s.at[j, c], tok_r.at[g, c], (dest, t, f))
+        side = remote(src, dst, side_s.at[j, c], tok_r.at[g, c], (dest, t, 1 - f))
+
+        @pl.when(dest != g)
+        def _():
+            away.wait_send() if end else away.start()
+
+        @pl.when(dest // 2 == beside_z)
+        def _():
+            side.wait_send() if end else side.start()
+
+        if not end:
+
+            @pl.when(dest == g)
+            def _():
+                pltpu.make_async_copy(src, dst, tok_r.at[g, c]).start()
+
     for c in range(PIECES):
         window = pl.ds(c * piece, piece)
         for j in range(blocks):
@@ -142,15 +173,7 @@
                 * gain_ref[:, cols].astype(jnp.float32)
             ).astype(jnp.bfloat16)
         for j in range(blocks):
-            dest = me * blocks + j
-
-            @pl.when(dest != g)
-            def _(c=c, j=j, dest=dest, window=window):
-                remote(sent.at[j, window], held.at[g, window], tok_s.at[j, c], tok_r.at[g, c], (dest, t, f)).start()
-
-            @pl.when(dest == g)
-            def _(c=c, j=j, window=window):
-                pltpu.make_async_copy(sent.at[j, window], held.at[g, window], tok_r.at[g, c]).start()
+            send_block(c, j, False)
 
     def order(i):
         return [0, *[d for k in range(1, line) for d in ((k, line - k) if k < line - k else (k,)) if k <= line - k]][i]
@@ -159,7 +182,7 @@
         across = remote(held.at[slot, window], held.at[slot, window], fx_s.at[k, c], tok_r.at[slot, c], mates[1])
         beside = remote(held.at[slot, window], held.at[slot, window], fc_s.at[k, c], tok_r.at[slot, c], mates[0])
 
-        @pl.when((t == owner_t) & (f == owner_f))
+        @pl.when((t == owner_t) & (f == owner_f) & (slot // 2 != beside_z))
         def _():
             across.wait_send() if end else across.start()
 
@@ -167,80 +190,176 @@
         def _():
             beside.wait_send() if end else beside.start()
 
-    def pair_copy(i):
-        return remote(pair_out.at[i], pair_in.at[i], pair_s.at[i], pair_r.at[i], (z * 2 + 1 - y, t, f))
-
-    def line_copy(i):
+    def pair_copy(i, c):
+        window = pl.ds(c * piece, piece)
         return remote(
-            line_out.at[i], line_in.at[i], line_s.at[i], line_r.at[i], (lax.rem(z + order(i), line) * 2 + y, t, f)
+            pair_out.at[i, window], pair_in.at[i, window], pair_s.at[i, c], pair_r.at[i, c], (z * 2 + 1 - y, t, f)
         )
 
-    def combine(i):
-        pair_copy(i).wait_recv()
-        both = total[i] + pair_in[i].astype(jnp.float32)
+    def line_copy(i, c):
+        window = pl.ds(c * piece, piece)
+        device = (lax.rem(z + order(i), line) * 2 + y, t, f)
+        return remote(line_out.at[i, window], line_in.at[i, window], line_s.at[i, c], line_r.at[i, c], device)
+
+    def combine(i, c):
+        window = pl.ds(c * piece, piece)
+        pair_copy(i, c).wait_recv()
+        both = total[i, window] + pair_in[i, window].astype(jnp.float32)
         if i == 0:
-            total[0] = both
+            total[0, window] = both
         else:
-            line_out[i] = both.astype(jnp.bfloat16)
-            line_copy(i).start()
-
-    for i in range(line):
-        zs = lax.rem(z + order(i), line)
-        for k, slot in enumerate((zs * 2 + 1 - y, zs * 2 + y)):
-            for c in range(PIECES):
-                window = pl.ds(c * piece, piece)
+            line_out[i, window] = both.astype(jnp.bfloat16)
+            line_copy(i, c).start()
+
+    batch_rows, slots, kv_width = k_ref.shape
+    steps = rows // batch_rows
+    kv_heads = kv_width // HEAD_SIZE
+    share = q_ref.shape[1] // kv_width
+    few = 128 // slots
+    band = few * steps
+    factor = HEAD_SIZE ** (-0.5)
+    chunks = batch_rows // few
+    over_last = (((1,), (1,)), ((), ()))
+
+    def head_lanes(x, h):
+        return pl.ds((x * share + h) * HEAD_SIZE, HEAD_SIZE)
+
+    def some_queries(b, x):
+        return jnp.concatenate([q_ref[pl.ds(b * band, band), head_lanes(x, h)] for h in range(share)], axis=0)
+
+    def attend_cached(b):
+        shape = (share * band, few * slots)
+        row = lax.rem(lax.broadcasted_iota(jnp.int32, shape, 0), band) // steps
+        same = row == lax.broadcasted_iota(jnp.int32, shape, 1) // slots
+        valid = same & (present_ref[pl.ds(b, 1), :] > 0.5)
+        for x in range(kv_heads):
+            lanes = pl.ds(x * HEAD_SIZE, HEAD_SIZE)
+            keys = k_ref[pl.ds(b * few, few), :, lanes].reshape(few * slots, HEAD_SIZE)
+            values = v_ref[pl.ds(b * few, few), :, lanes].reshape(few * slots, HEAD_SIZE)
+            scores = (
+                lax.dot_general(some_queries(b, x), keys, over_last, preferred_element_type=jnp.float32) * factor
+            )
+            scores = jnp.where(valid, scores, -jnp.inf)
+            most = jnp.max(scores, axis=1, keepdims=True)
+            probs = jnp.exp(scores - most)
+            part_max[b, x] = jnp.broadcast_to(most, (share * band, HEAD_SIZE))
+            part_sum[b, x] = jnp.broadcast_to(jnp.sum(probs, axis=1, keepdims=True), (share * band, HEAD_SIZE))
+            part_out[b, x] = jnp.dot(probs.astype(jnp.bfloat16), values, preferred_element_type=jnp.float32)
+
+    def attend_new(b):
+        shape = (share * band, band)
+        mine = lax.rem(lax.broadcasted_iota(jnp.int32, shape, 0), band)
+        other = lax.broadcasted_iota(jnp.int32, shape, 1)
+        valid = (mine // steps == other // steps) & (other <= mine)
+        window = pl.ds(b * band, band)
+        for x in range(kv_heads):
+            keys = app_ref[window, pl.ds(2 * x * HEAD_SIZE, HEAD_SIZE)]
+            values = app_ref[window, pl.ds((2 * x + 1) * HEAD_SIZE, HEAD_SIZE)]
+            scores = (
+                lax.dot_general(some_queries(b, x), keys, over_last, preferred_element_type=jnp.float32) * factor
+            )
+            scores = jnp.where(valid, scores, -jnp.inf)
+            before = part_max[b, x]
+            most = jnp.maximum(before, jnp.max(scores, axis=1, keepdims=True))
+            probs = jnp.exp(scores - most[:, :1])
+            again = jnp.exp(before - most)
+            denom = again * part_sum[b, x] + jnp.sum(probs, axis=1, keepdims=True)
+            blended = again * part_out[b, x] + jnp.dot(
+                probs.astype(jnp.bfloat16), values, preferred_element_type=jnp.float32
+            )
+            blended = (blended / denom).astype(jnp.bfloat16)
+            for h in range(share):
+                out_ref[window, head_lanes(x, h)] = blended[h * band : (h + 1) * band]
+
+    late = None
+    done = 0
+    for c in range(PIECES):
+        window = pl.ds(c * piece, piece)
+        for i in range(line):
+            zs = lax.rem(z + order(i), line)
+            for k, slot in enumerate((zs * 2 + 1 - y, zs * 2 + y)):
                 remote(
                     held.at[slot, window], held.at[slot, window], fx_s.at[0, 0], tok_r.at[slot, c], mates[1]
                 ).wait_recv()
                 forward(slot, window, 2 * i + k, c, False)
-            product = jnp.dot(held[slot], w_ref[...], preferred_element_type=jnp.float32)
-            if k == 0:
-                pair_out[i] = product.astype(jnp.bfloat16)
-                pair_copy(i).start()
-            else:
-                total[i] = product
-        if i > 0:
-            combine(i - 1)
-    combine(line - 1)
-    result = total[0]
-    for i in range(1, line):
-        line_copy(i).wait_recv()
-        result = result + line_in[i].astype(jnp.float32)
-    o_ref[...] = result
-
+                product = jnp.dot(held[slot, window], w_ref[...], preferred_element_type=jnp.float32)
+                if k == 0:
+                    pair_out[i, window] = product.astype(jnp.bfloat16)
+                    pair_copy(i, c).start()
+                else:
+                    total[i, window] = product
+            if late is not None:
+                combine(*late)
+            late = (i, c)
+            if c == 0 and i == 0:
+                for copy in loads:
+                    copy.wait()
+            steps_now = -(-chunks // (line * PIECES))
+            for b in range(done, min(done + steps_now, chunks)):
+                attend_cached(b)
+            done = min(done + steps_now, chunks)
+    combine(*late)
+
+    half = HEAD_SIZE // 2
     for c in range(PIECES):
         window = pl.ds(c * piece, piece)
+        result = total[0, window]
+        for i in range(1, line):
+            line_copy(i, c).wait_recv()
+            result = result + line_in[i, window].astype(jnp.float32)
+        for x in range(kv_heads):
+            key = result[:, 2 * x * HEAD_SIZE : (2 * x + 1) * HEAD_SIZE]
+            key = key * cos_ref[window, :] + pltpu.roll(key, half, 1) * sin_ref[window, :]
+            app_ref[window, pl.ds(2 * x * HEAD_SIZE, HEAD_SIZE)] = key.astype(jnp.bfloat16)
+            app_ref[window, pl.ds((2 * x + 1) * HEAD_SIZE, HEAD_SIZE)] = result[
+                :, (2 * x + 1) * HEAD_SIZE : (2 * x + 2) * HEAD_SIZE
+            ].astype(jnp.bfloat16)
+        for b in range(c * chunks // PIECES, (c + 1) * chunks // PIECES):
+            attend_new(b)
+
+    for c in range(PIECES):
         for j in range(blocks):
-            dest = me * blocks + j
-
-            @pl.when(dest != g)
-            def _(c=c, j=j, dest=dest, window=window):
-                remote(
-                    sent.at[j, window], held.at[g, window], tok_s.at[j, c], tok_r.at[g, c], (dest, t, f)
-                ).wait_send()
-
-    for i in range(line):
-        zs = lax.rem(z + order(i), line)
-        for k, slot in enumerate((zs * 2 + 1 - y, zs * 2 + y)):
-            for c in range(PIECES):
+            send_block(c, j, True)
+        for i in range(line):
+            zs = lax.rem(z + order(i), line)
+            for k, slot in enumerate((zs * 2 + 1 - y, zs * 2 + y)):
                 forward(slot, pl.ds(c * piece, piece), 2 * i + k, c, True)
-        pair_copy(i).wait_send()
-        if i > 0:
-            line_copy(i).wait_send()
-
-
-def exchange(sizes, tokens, gain, layer):
+            pair_copy(i, c).wait_send()
+            if i > 0:
+                line_copy(i, c).wait_send()
+
+
+def project_and_attend(sizes, tokens, norm_gain, layer, queries, key_cache, value_cache, lengths):
     grp, _, _ = sizes
-    rows, width = tokens.shape
+    batch_rows, steps, width = tokens.shape
+    _, slots, kv_width = key_cache.shape
+    rows = batch_rows * steps
     depth, columns = layer.shape
     blocks, line = width // depth, grp // 2
+    kv_heads, share = kv_width // HEAD_SIZE, queries.shape[2] // kv_width
+    few = 128 // slots
+    half = HEAD_SIZE // 2
+    positions = (lengths[:, None] + jnp.arange(steps, dtype=jnp.int32)[None, :]).astype(jnp.float32)
+    frequency = rope_base ** (-(jnp.arange(half, dtype=jnp.float32) * 2.0 / HEAD_SIZE))
+    angles = positions.reshape(rows, 1) * frequency[None, :]
+    cosine, sine = jnp.cos(angles), jnp.sin(angles)
+    cosine = jnp.concatenate([cosine, cosine], axis=1)
+    sine = jnp.concatenate([-sine, sine], axis=1)
+    present = (jnp.arange(slots, dtype=jnp.int32)[None, :] < lengths[:, None]).astype(jnp.float32)
+    present = present.reshape(batch_rows // few, few * slots)
     dma = pltpu.SemaphoreType.DMA
     vmem = pl.BlockSpec(memory_space=pltpu.VMEM)
-    return pl.pallas_call(
+    anywhere = pl.BlockSpec(memory_space=pl.ANY)
+    flat_queries = queries.reshape(rows, queries.shape[2])
+    part = pltpu.VMEM((batch_rows // few, kv_heads, share * few * steps, HEAD_SIZE), jnp.float32)
+    attended, appended = pl.pallas_call(
         functools.partial(exchange_kernel, sizes),
-        out_shape=jax.ShapeDtypeStruct((rows, columns), jnp.float32),
-        in_specs=[vmem] * 3,
-        out_specs=vmem,
+        out_shape=(
+            jax.ShapeDtypeStruct(flat_queries.shape, jnp.bfloat16),
+            jax.ShapeDtypeStruct((rows, columns), jnp.bfloat16),
+        ),
+        in_specs=[vmem] * 6 + [anywhere] * 3,
+        out_specs=(vmem, vmem),
         scratch_shapes=[
             pltpu.VMEM((blocks, rows, depth), jnp.bfloat16),
             pltpu.VMEM((grp, rows, depth), jnp.bfloat16),
@@ -251,32 +370,45 @@
             pltpu.VMEM((line, rows, columns), jnp.float32),
             pltpu.VMEM((line, rows, columns), jnp.bfloat16),
             pltpu.VMEM((line, rows, columns), jnp.bfloat16),
+            pltpu.VMEM(flat_queries.shape, jnp.bfloat16),
+            pltpu.VMEM(key_cache.shape, jnp.bfloat16),
+            pltpu.VMEM(value_cache.shape, jnp.bfloat16),
+            part,
+            part,
+            part,
             dma((3,)),
             dma((3,)),
             dma((blocks, PIECES)),
             dma((grp, PIECES)),
             dma((grp, PIECES)),
             dma((grp, PIECES)),
-            dma((line,)),
-            dma((line,)),
-            dma((line,)),
-            dma((line,)),
+            dma((blocks, PIECES)),
+            dma((line, PIECES)),
+            dma((line, PIECES)),
+            dma((line, PIECES)),
+            dma((line, PIECES)),
+            dma((3,)),
         ],
         compiler_params=pltpu.CompilerParams(collective_id=0, has_side_effects=True, vmem_limit_bytes=48 << 20),
-    )(tokens, gain, layer)
-
-
-def project(sizes, tokens, norm_gain, layer_half):
+    )(
+        tokens.reshape(rows, width), norm_gain.reshape(1, width), layer, cosine, sine, present, flat_queries, key_cache,
+        value_cache,
+    )
+    return attended.reshape(queries.shape), appended.reshape(batch_rows, steps, columns)
+
+
+def fits(sizes, tokens, layer_half, queries, key_cache):
+    grp, tp, fs = sizes
     batch_rows, steps, width = tokens.shape
-    return exchange(sizes, tokens.reshape(batch_rows * steps, width), norm_gain.reshape(1, width), layer_half)
-
-
-def fits(sizes, tokens, layer_half):
-    grp, tp, fs = sizes
-    rows, width, depth = tokens.shape[0] * tokens.shape[1], tokens.shape[2], layer_half.shape[0]
+    rows, depth, columns = batch_rows * steps, layer_half.shape[0], layer_half.shape[1]
+    slots, kv_width = key_cache.shape[1:]
+    if tp != 2 or fs != 2 or grp % 4 or not 4 <= grp <= 16 or 128 % slots or slots % 16:
+        return False
+    few = 128 // slots
     return (
-        tp == 2 and fs == 2 and grp % 2 == 0 and 4 <= grp <= 16 and depth % 128 == 0 and width % depth == 0
-        and rows % (128 * PIECES) == 0 and layer_half.shape[1] % 128 == 0
+        depth % 128 == 0 and width % depth == 0 and rows % 128 == 0 and rows % (16 * PIECES) == 0
+        and columns == 2 * kv_width and few * steps % 16 == 0 and batch_rows % (few * PIECES) == 0
+        and queries.shape[2] % kv_width == 0
     )
 
 
@@ -318,10 +450,12 @@
     layer_half = renewed.astype(jnp.bfloat16)
     batch_rows, steps = (tokens.shape[0], tokens.shape[1])
     columns = layer_half.shape[1]
-    if fits(sizes, tokens, layer_half):
-        projected_output = project(sizes, tokens, norm_gain, layer_half)
-    else:
-        projected_output = project_gathered(tokens, norm_gain, layer_half)
+    if fits(sizes, tokens, layer_half, queries, rotated_key_cache):
+        attended, appended = project_and_attend(
+            sizes, tokens, norm_gain, layer_half, queries, rotated_key_cache, head_value_cache, lengths
+        )
+        return (attended, appended, renewed, average, variance)
+    projected_output = project_gathered(tokens, norm_gain, layer_half)
     kv_heads = columns // (2 * HEAD_SIZE)
     projected_output = projected_output.reshape(batch_rows, steps, kv_heads, 2, HEAD_SIZE)
     positions = (lengths[:, None] + jnp.arange(steps, dtype=jnp.int32)[None, :]).astype(jnp.float32)

time: 124 us -> 105 us (0.85)
  matrix products: 10.7 us -> 0 us
  other arithmetic: 11.9 us -> 8.85 us
  Pallas kernels: 91.4 us -> 88.4 us
  local copies, waits for them, and re-layouts: 8.85 us -> 6.14 us
    dot_general x4 -> x0, matrix products: 10.7 us -> none  [the longest x1 4.8 us: attention(): jnp.einsum('rsxgd,ruxd->rxgsu', query_heads, key_new, preferred_element_t...]
    pallas_call x1, Pallas kernels: 91.4 us -> 88.4 us  [project_and_attend(): pl.pallas_call(functools.partial(exchange_kernel, sizes), out_shape=(jax....]
    reduce_sum x2 -> x0, other arithmetic: 2.37 us -> none  [the longest x1 1.4 us: attention(): jnp.sum(probs_cached, axis=-1, keepdims=True)]
    unnamed x24 -> x8, local copies, waits for them, and re-layouts: 2.55 us -> 0.71 us
    reshape x6 -> x5, local copies, waits for them, and re-layouts: 5.84 us -> 4.34 us  [the longest x1 1.34 us: project_and_attend(): tokens.reshape(rows, width)]
where the time goes in v2:
time: 105 us; the launch traced here: 104 us
  Pallas kernels  88.4 us (84%)
  other arithmetic  8.85 us (8%)
  local copies, waits for them, and re-layouts  6.14 us (6%)
    pallas_call x1, Pallas kernels, project_and_attend(): pl.pallas_call(functools.partial(exchange_kernel, sizes), out_shape=(jax....  88.4 us
    convert_element_type x1, other arithmetic, shards(): layer_half = renewed.astype(jnp.bfloat16)  7.42 us

profile of v2, /device:TPU:2, one launch (start us, length us, event | category | flops | bytes accessed | tf_op | source)
XLA Modules:
  0.0 104.1 jit_solution(6438728906149905403)
XLA Ops:
  0.6 0.0 copy-start.3
  0.7 0.1 lt.23
  0.7 0.8 reshape.54.gain_ref
  1.5 0.7 lt.25
  2.2 0.1 lt.26
  2.3 0.1 lt.27
  2.4 0.7 add_convert_fusion
  3.2 0.1 convert_element_type.19
  3.3 0.5 fusion.1
  3.8 0.1 pad_maximum_fusion
  4.0 1.3 %reshape.53.tok_ref = bf16[256,2048]{1,0:T(8,128)(2,1)S(1)} reshape(bf16[64,4,2048]{2,1,0:T(4,128)(2,1)} %param.10) | data formatting | bytes 2097152 | tf_op jit(solution)/shard_map/reshape | solution.py:394
  5.3 0.0 copy-done.3
  5.3 0.3 reshape.55.q_hbm
  5.6 0.0 copy-start
  5.6 7.4 %fusion.2 = (bf16[1024,512]{1,0:T(8,128)(2,1)S(1)}, f32[1024,512]{1,0:T(8,128)}, f32[1024,512]{1,0:T(8,128)}, f32[1024,512]{1,0:T(8,128)}) fusion(f32[1024,512]{1,0:T(8,128)} %param.16, f32[1024,512]{1,0:T(8,128)} %param.19, f32[1024,512]{1,0:T(8,128)} %param.17, f32[1024,512]{1,0:T(8,128)} %param.18), kind=kLoop, calls=%fused_computation.12 | loop fusion | flops 8388608 | bytes 15728640 | tf_op jit(solution)/shard_map/convert_element_type | solution.py:450
  13.0 0.0 copy-done
  13.0 88.4 %shard_map.137 = (bf16[256,2048]{1,0:T(8,128)(2,1)S(1)}, bf16[256,512]{1,0:T(8,128)(2,1)S(1)}) custom-call(bf16[256,2048]{1,0:T(8,128)(2,1)S(1)} %reshape.53.tok_ref, bf16[1,2048]{1,0:T(2,128)(2,1)S(1)} %reshape.54.gain_ref, bf16[1024,512]{1,0:T(8,128)(2,1)S(1)} %get-tuple-element.9.w_ref, f32[256,128]{1,0:T(8,128)S(1)} %get-tuple-element.16.cos_ref, ...), custom_call_target="tpu_custom_call" | custom-call | tf_op jit(solution)/shard_map/pallas_call | solution.py:355
  101.5 0.0 copy-start.1
  101.5 0.7 copy-done.1
  102.2 0.0 copy-start.2
  102.2 1.2 %reshape.56 = bf16[64,4,2048]{2,1,0:T(4,128)(2,1)} reshape(bf16[256,2048]{1,0:T(8,128)(2,1)S(1)} %get-tuple-element.7) | data formatting | bytes 2097152 | tf_op jit(solution)/shard_map/reshape | solution.py:397
  103.4 0.0 copy-done.2
  103.4 0.8 reshape.57
  (3 shorter events, 0.0 us)
Async XLA Ops:
  0.6 4.7 %copy-start.3 = (bf16[64,4,2048]{2,1,0:T(4,128)(2,1)S(1)}, bf16[64,4,2048]{2,1,0:T(4,128)(2,1)}, u32[]{:S(2)}) copy-start(bf16[64,4,2048]{2,1,0:T(4,128)(2,1)} %param.12) | copy-start | bytes 3145732
  5.6 7.4 %copy-start = (bf16[64,32,256]{2,1,0:T(8,128)(2,1)S(1)}, bf16[64,32,256]{2,1,0:T(8,128)(2,1)}, u32[]{:S(2)}) copy-start(bf16[64,32,256]{2,1,0:T(8,128)(2,1)} %k_hbm.1) | copy-start | bytes 3145732
  101.5 0.7 copy-start.1
  102.2 1.2 %copy-start.2 = (bf16[256,512]{1,0:T(8,128)(2,1)S(1)}, bf16[256,512]{1,0:T(8,128)(2,1)}, u32[]{:S(2)}) copy-start(bf16[256,512]{1,0:T(8,128)(2,1)} %copy-done.1) | copy-start | bytes 786436

commit v3 on v2

--- a/solution.py
+++ b/solution.py
@@ -93,7 +93,7 @@
 
 def exchange_kernel(sizes, tok_ref, gain_ref, w_ref, cos_ref, sin_ref, present_ref, q_hbm, k_hbm, v_hbm, out_ref, app_ref,
                     sent, held, squares, squares_in, pair_out, pair_in, total, line_out, line_in, q_ref, k_ref, v_ref,
-                    part_out, part_max, part_sum, sq_s, sq_r, tok_s, tok_r, fx_s, fc_s, side_s, pair_s, pair_r, line_s, line_r,
+                    part_out, part_max, part_sum, sq_s, sq_r, tok_s, tok_r, fx_s, fc_s, pair_s, pair_r, line_s, line_r,
                     load_s):
     grp, tp, fs = sizes
     line = grp // 2
@@ -115,15 +115,13 @@
     barrier = pltpu.get_barrier_semaphore()
     peers = [(lax.rem(g + i, grp), t, f) for i in range(1, grp)]
     mates = [(g, 1 - t, f), (g, t, 1 - f), (g, 1 - t, 1 - f)]
-    beside_z = z + 1 - 2 * lax.rem(z, 2)
-    sides = [(beside_z * 2 + i, t, 1 - f) for i in range(2)]
     loads = [
         pltpu.make_async_copy(src, dst, load_s.at[i])
         for i, (src, dst) in enumerate(((q_hbm, q_ref), (k_hbm, k_ref), (v_hbm, v_ref)))
     ]
     for copy in loads:
         copy.start()
-    for device in peers + mates + sides:
+    for device in peers + mates:
         pl.semaphore_signal(barrier, inc=1, device_id=device, device_id_type=MESH_ID)
 
     wide = tok_ref[...].astype(jnp.float32)
@@ -132,7 +130,7 @@
     for i in range(1, width // 128):
         part = part + wide[:, i * 128 : (i + 1) * 128]
     squares[...] = jnp.broadcast_to(jnp.sum(part.T, axis=0, keepdims=True), squares.shape)
-    pl.semaphore_wait(barrier, len(peers) + len(mates) + len(sides))
+    pl.semaphore_wait(barrier, len(peers) + len(mates))
     sq = [remote(squares, squares_in.at[i], sq_s.at[i], sq_r.at[i], mates[i]) for i in range(3)]
     for copy in sq:
         copy.start()
@@ -147,15 +145,10 @@
         window = pl.ds(c * piece, piece)
         src, dst = sent.at[j, window], held.at[g, window]
         away = remote(src, dst, tok_s.at[j, c], tok_r.at[g, c], (dest, t, f))
-        side = remote(src, dst, side_s.at[j, c], tok_r.at[g, c], (dest, t, 1 - f))
 
         @pl.when(dest != g)
         def _():
             away.wait_send() if end else away.start()
-
-        @pl.when(dest // 2 == beside_z)
-        def _():
-            side.wait_send() if end else side.start()
 
         if not end:
 
@@ -172,8 +165,9 @@
                 * scale[c * piece : (c + 1) * piece]
                 * gain_ref[:, cols].astype(jnp.float32)
             ).astype(jnp.bfloat16)
-        for j in range(blocks):
-            send_block(c, j, False)
+        if c < 1:
+            for j in range(blocks):
+                send_block(c, j, False)
 
     def order(i):
         return [0, *[d for k in range(1, line) for d in ((k, line - k) if k < line - k else (k,)) if k <= line - k]][i]
@@ -182,11 +176,13 @@
         across = remote(held.at[slot, window], held.at[slot, window], fx_s.at[k, c], tok_r.at[slot, c], mates[1])
         beside = remote(held.at[slot, window], held.at[slot, window], fc_s.at[k, c], tok_r.at[slot, c], mates[0])
 
-        @pl.when((t == owner_t) & (f == owner_f) & (slot // 2 != beside_z))
+        lead = owner_t if c % 2 == 0 else 1 - owner_t
+
+        @pl.when((t == lead) & (f == owner_f))
         def _():
             across.wait_send() if end else across.start()
 
-        @pl.when(t == owner_t)
+        @pl.when(((f == owner_f) & (t == owner_t)) | ((f != owner_f) & (t == lead)))
         def _():
             beside.wait_send() if end else beside.start()
 
@@ -275,9 +271,14 @@
     done = 0
     for c in range(PIECES):
         window = pl.ds(c * piece, piece)
+        if c + 1 < PIECES:
+            for j in range(blocks):
+                send_block(c, j, True)
+                send_block(c + 1, j, False)
         for i in range(line):
             zs = lax.rem(z + order(i), line)
-            for k, slot in enumerate((zs * 2 + 1 - y, zs * 2 + y)):
+            visits = ((0, zs * 2 + 1 - y), (1, zs * 2 + y))
+            for k, slot in visits if i else visits[::-1]:
                 remote(
                     held.at[slot, window], held.at[slot, window], fx_s.at[0, 0], tok_r.at[slot, c], mates[1]
                 ).wait_recv()
@@ -319,7 +320,8 @@
 
     for c in range(PIECES):
         for j in range(blocks):
-            send_block(c, j, True)
+            if c + 1 >= PIECES:
+                send_block(c, j, True)
         for i in range(line):
             zs = lax.rem(z + order(i), line)
             for k, slot in enumerate((zs * 2 + 1 - y, zs * 2 + y)):
@@ -382,7 +384,6 @@
             dma((grp, PIECES)),
             dma((grp, PIECES)),
             dma((grp, PIECES)),
-            dma((blocks, PIECES)),
             dma((line, PIECES)),
             dma((line, PIECES)),
             dma((line, PIECES)),

time: 105 us -> 98.1 us (0.934)
  Pallas kernels: 88.4 us -> 81 us
    pallas_call x1, Pallas kernels: 88.4 us -> 81 us  [project_and_attend(): pl.pallas_call(functools.partial(exchange_kernel, sizes), out_shape=(jax....]
where the time goes in v3:
time: 98.1 us; the launch traced here: 96.7 us
  Pallas kernels  81 us (83%)
  other arithmetic  8.85 us (9%)
  local copies, waits for them, and re-layouts  6.14 us (6%)
    pallas_call x1, Pallas kernels, project_and_attend(): pl.pallas_call(functools.partial(exchange_kernel, sizes), out_shape=(jax....  81 us
    convert_element_type x1, other arithmetic, shards(): layer_half = renewed.astype(jnp.bfloat16)  7.42 us

profile of v3, /device:TPU:2, one launch (start us, length us, event | category | flops | bytes accessed | tf_op | source)
XLA Modules:
  0.0 96.7 jit_solution(8534122164553685985)
XLA Ops:
  0.6 0.0 copy-start.3
  0.7 0.1 lt.23
  0.7 0.8 reshape.54.gain_ref
  1.5 0.7 lt.25
  2.2 0.1 lt.26
  2.3 0.1 lt.27
  2.4 0.7 add_convert_fusion
  3.2 0.1 convert_element_type.19
  3.3 0.5 fusion.1
  3.8 0.1 pad_maximum_fusion
  4.0 1.3 %reshape.53.tok_ref = bf16[256,2048]{1,0:T(8,128)(2,1)S(1)} reshape(bf16[64,4,2048]{2,1,0:T(4,128)(2,1)} %param.10) | data formatting | bytes 2097152 | tf_op jit(solution)/shard_map/reshape | solution.py:395
  5.3 0.0 copy-done.3
  5.3 0.3 reshape.55.q_hbm
  5.6 0.0 copy-start
  5.6 7.4 %fusion.2 = (bf16[1024,512]{1,0:T(8,128)(2,1)S(1)}, f32[1024,512]{1,0:T(8,128)}, f32[1024,512]{1,0:T(8,128)}, f32[1024,512]{1,0:T(8,128)}) fusion(f32[1024,512]{1,0:T(8,128)} %param.16, f32[1024,512]{1,0:T(8,128)} %param.19, f32[1024,512]{1,0:T(8,128)} %param.17, f32[1024,512]{1,0:T(8,128)} %param.18), kind=kLoop, calls=%fused_computation.12 | loop fusion | flops 8388608 | bytes 15728640 | tf_op jit(solution)/shard_map/convert_element_type | solution.py:451
  13.0 0.0 copy-done
  13.0 81.0 %shard_map.137 = (bf16[256,2048]{1,0:T(8,128)(2,1)S(1)}, bf16[256,512]{1,0:T(8,128)(2,1)S(1)}) custom-call(bf16[256,2048]{1,0:T(8,128)(2,1)S(1)} %reshape.53.tok_ref, bf16[1,2048]{1,0:T(2,128)(2,1)S(1)} %reshape.54.gain_ref, bf16[1024,512]{1,0:T(8,128)(2,1)S(1)} %get-tuple-element.9.w_ref, f32[256,128]{1,0:T(8,128)S(1)} %get-tuple-element.16.cos_ref, ...), custom_call_target="tpu_custom_call" | custom-call | tf_op jit(solution)/shard_map/pallas_call | solution.py:357
  94.1 0.0 copy-start.1
  94.1 0.7 copy-done.1
  94.8 0.0 copy-start.2
  94.8 1.2 %reshape.56 = bf16[64,4,2048]{2,1,0:T(4,128)(2,1)} reshape(bf16[256,2048]{1,0:T(8,128)(2,1)S(1)} %get-tuple-element.7) | data formatting | bytes 2097152 | tf_op jit(solution)/shard_map/reshape | solution.py:398
  96.0 0.0 copy-done.2
  96.0 0.8 reshape.57
  (3 shorter events, 0.0 us)
Async XLA Ops:
  0.6 4.7 %copy-start.3 = (bf16[64,4,2048]{2,1,0:T(4,128)(2,1)S(1)}, bf16[64,4,2048]{2,1,0:T(4,128)(2,1)}, u32[]{:S(2)}) copy-start(bf16[64,4,2048]{2,1,0:T(4,128)(2,1)} %param.12) | copy-start | bytes 3145732
  5.6 7.4 %copy-start = (bf16[64,32,256]{2,1,0:T(8,128)(2,1)S(1)}, bf16[64,32,256]{2,1,0:T(8,128)(2,1)}, u32[]{:S(2)}) copy-start(bf16[64,32,256]{2,1,0:T(8,128)(2,1)} %k_hbm.1) | copy-start | bytes 3145732
  94.1 0.7 copy-start.1
  94.8 1.2 %copy-start.2 = (bf16[256,512]{1,0:T(8,128)(2,1)S(1)}, bf16[256,512]{1,0:T(8,128)(2,1)}, u32[]{:S(2)}) copy-start(bf16[256,512]{1,0:T(8,128)(2,1)} %copy-done.1) | copy-start | bytes 786436
